TPU v7x, 128 devices: a whole 4x4x4 slice. The times are simulated.
128 devices in a mesh: row: 16 (over x_hi, y, core), proto: 8 (over z, x_lo).
Axes of the slice: x: 4 (x_hi: 2, x_lo: 2; x = x_hi * 2 + x_lo), y: 4, z: 4, core: 2. Of those that a mesh axis runs over, the one named last changes fastest.
Arguments:
- tokens: bfloat16 [8192, 4096], P('row'), may hold values from -6 to 6
- w_in: bfloat16 [4096, 8192], P('row', 'proto'), may hold values from -0.09375 to 0.09375
- w_out: bfloat16 [8192, 384], P('proto'), may hold values from -0.0625 to 0.0625
- teacher_z: bfloat16 [8192, 384], P(('row', 'proto')), may hold values from -6 to 6
- proto_student: bfloat16 [384, 49152], P(None, 'proto'), may hold values from -48 to 48
- proto_teacher: bfloat16 [384, 49152], P(None, 'proto'), may hold values from -48 to 48
- center: float32 [49152], P('proto'), may hold values from -0.6 to 0.6
- image_of: int32 [8192], P('row'), may hold values from 0 to 63
Outputs:
- loss: float32 [], replicated
- w_in_grad: float32 [4096, 8192], P('row', 'proto')
- w_out_grad: float32 [8192, 384], P('proto')
- proto_grad: float32 [384, 49152], P('row', 'proto')
All inputs are finite; a program needn't handle non-finite values.
Results may differ from a plain program's by a relative error of at most 0.015.
Values may be sent and summed in bfloat16 or wider, within the bound.
A program may use at most 128 MiB of HBM per device.

v0:
```python
import jax
import jax.numpy as jnp
from jax import lax
from jax.sharding import PartitionSpec as P

tau_teacher = 0.07
tau_student = 0.1
loss_scale = 1048576.0
norm_eps = 1e-06


def gelu_parts(values):
    cumul = 0.5 * (1.0 + jax.scipy.special.erf(values * 0.7071067811865476))
    density = jnp.exp(-0.5 * values * values) * 0.3989422804014327
    return (values * cumul, cumul + values * density)


def inner(left, right):
    return lax.dot_general(
        left, right, (((0,), (0,)), ((), ())), preferred_element_type=jnp.float32
    )


def outer_last(left, right):
    return lax.dot_general(
        left, right, (((1,), (1,)), ((), ())), preferred_element_type=jnp.float32
    )


def normalize(values):
    recip = lax.rsqrt(jnp.sum(values * values, axis=1, keepdims=True) + norm_eps)
    return (recip, values * recip)


def teacher_norm(teacher_z):
    teach = teacher_z.astype(jnp.float32)
    return (teach * lax.rsqrt(jnp.sum(teach * teach, axis=1, keepdims=True) + norm_eps)).astype(
        jnp.bfloat16
    )


def back_norm(dnorm, recip, unit):
    return (recip * (dnorm - unit * jnp.sum(unit * dnorm, axis=1, keepdims=True))).astype(
        jnp.bfloat16
    )


def on_device(tokens, w_in, w_out, teacher_z, proto_student, proto_teacher, center, image_of):
    row_count = tokens.shape[0]
    images = row_count * lax.axis_size("row") // 128
    onehot = (image_of[:, None] == jnp.arange(images, dtype=jnp.int32)[None, :]).astype(jnp.float32)
    counts = lax.psum(jnp.sum(onehot, axis=0), "row")
    weight = 1.0 / (images * jnp.sum(onehot * counts[None, :], axis=1))
    pre = jnp.dot(
        tokens, lax.all_gather(w_in, "row", axis=0, tiled=True), preferred_element_type=jnp.float32
    )
    act, slope = gelu_parts(pre)
    hidden = act.astype(jnp.bfloat16)
    partial_value = jnp.dot(hidden, w_out, preferred_element_type=jnp.float32)
    bott = lax.psum(partial_value, "proto")
    recip, unit = normalize(bott)
    student_n = unit.astype(jnp.bfloat16)
    teacher_n = lax.all_gather(teacher_norm(teacher_z), "proto", axis=0, tiled=True)
    logit_t = (
        jnp.dot(teacher_n, proto_teacher, preferred_element_type=jnp.float32) - center[None, :]
    ) / tau_teacher
    logit_s = jnp.dot(student_n, proto_student, preferred_element_type=jnp.float32) / tau_student
    local_t = jnp.max(logit_t, axis=1)
    local_s = jnp.max(logit_s, axis=1)
    top_t, top_s = lax.pmax((local_t, local_s), "proto")
    exp_t = jnp.exp(logit_t - top_t[:, None])
    exp_s = jnp.exp(logit_s - top_s[:, None])
    total_t, total_s = lax.psum((jnp.sum(exp_t, axis=1), jnp.sum(exp_s, axis=1)), "proto")
    prob_t = exp_t / total_t[:, None]
    prob_s = exp_s / total_s[:, None]
    logp_s = logit_s - top_s[:, None] - jnp.log(total_s)[:, None]
    cross = -jnp.sum(prob_t * logp_s, axis=1)
    loss = lax.psum(jnp.sum(weight * cross), ("row", "proto"))
    grad_s = (loss_scale * weight[:, None] * (prob_s - prob_t) / tau_student).astype(jnp.bfloat16)
    proto_grad = lax.psum_scatter(
        inner(student_n, grad_s).astype(jnp.bfloat16), "row", scatter_dimension=0, tiled=True
    ).astype(jnp.float32)
    dnorm_part = outer_last(grad_s, proto_student)
    dnorm = lax.psum(dnorm_part, "proto")
    dbott = back_norm(dnorm, recip, unit)
    w_out_grad = lax.psum(inner(hidden, dbott).astype(jnp.bfloat16), "row").astype(jnp.float32)
    dpre = (outer_last(dbott, w_out) * slope).astype(jnp.bfloat16)
    w_in_grad = lax.psum_scatter(
        inner(tokens, dpre).astype(jnp.bfloat16), "row", scatter_dimension=0, tiled=True
    ).astype(jnp.float32)
    return (loss, w_in_grad, w_out_grad, proto_grad)


def solution(mesh):
    return jax.shard_map(
        on_device,
        mesh=mesh,
        in_specs=(
            P("row", None),
            P("row", "proto"),
            P("proto", None),
            P(("row", "proto"), None),
            P(None, "proto"),
            P(None, "proto"),
            P("proto"),
            P("row"),
        ),
        out_specs=(P(), P("row", "proto"), P("proto", None), P("row", "proto")),
        check_vma=False,
    )
```

profile of v0, /device:TPU:0, one launch (start us, length us, event | category | flops | bytes accessed | tf_op | source)
XLA Modules:
  0.0 676.0 jit_solution(12270464372114535581)
XLA Ops:
  8.8 38.4 %psum.49 = f32[64]{0:T(128)S(1)} all-reduce(f32[64]{0:T(128)S(1)} %convert_reduce_fusion), channel_id=1, replica_groups=mesh['row'=16,'proto'=8] {'row'}, use_global_device_ids=true, to_apply=%region_1.0 | all-reduce | flops 64 | bytes 512 | tf_op jit(solution)/shard_map/psum | solution.py:52
  49.8 35.8 %all-gather.2.cloned.1.call-done = bf16[4096,1024]{1,0:T(8,128)(2,1)} async-done(((bf16[256,1024]{1,0:T(8,128)(2,1)}), bf16[4096,1024]{1,0:T(8,128)(2,1)}) %all-gather.2.cloned.1.call-update) | async-done | bytes 8388624 | tf_op jit(solution)/shard_map/all_gather | solution.py:55
  85.6 10.6 %multiply_convert_fusion.1 = (bf16[512,1024]{1,0:T(8,128)(2,1)S(1)}, f32[512,1024]{1,0:T(8,128)}) fusion(bf16[512,4096]{1,0:T(8,128)(2,1)} %param.8, bf16[4096,1024]{1,0:T(8,128)(2,1)} %all-gather.2.cloned.1.call-done), kind=kOutput, calls=%fused_computation.19 | convolution fusion | flops 4297588736 | bytes 15728640 | tf_op jit(solution)/shard_map/dot_general | solution.py:54
  97.8 31.3 %all_gather.6 = bf16[512,384]{1,0:T(8,128)(2,1)S(1)} all-gather(bf16[64,384]{1,0:T(8,128)(2,1)S(1)} %fusion.10), channel_id=1, replica_groups=mesh['row'=16,'proto'=8] {'proto'}, dimensions={0}, use_global_device_ids=true | all-gather | bytes 442368 | tf_op jit(solution)/shard_map/all_gather | solution.py:63
  129.1 9.0 %fusion = (f32[512]{0:T(512)S(1)}, f32[512,6144]{1,0:T(8,128)}) fusion(f32[6144]{0:T(1024)S(1)} %copy-done.3, bf16[512,384]{1,0:T(8,128)(2,1)S(1)} %all_gather.6, bf16[384,6144]{1,0:T(8,128)(2,1)} %param.13), kind=kOutput, calls=%fused_computation.7 | convolution fusion | flops 2425355776 | bytes 17721344 | tf_op jit(solution)/shard_map/dot_general | solution.py:65
  138.2 37.0 %all-reduce.6.cloned.1.call-done = f32[512,384]{1,0:T(8,128)} async-done(((f32[512,384]{1,0:T(8,128)}), f32[512,384]{1,0:T(8,128)}) %all-reduce.6.cloned.1.call-update) | async-done | bytes 786448 | tf_op jit(solution)/shard_map/psum | solution.py:60
  176.5 10.6 %multiply_reduce_fusion.1 = (f32[512]{0:T(512)S(1)}, f32[512,6144]{1,0:T(8,128)}) fusion(bf16[384,6144]{1,0:T(8,128)(2,1)} %param.12, f32[512,384]{1,0:T(8,128)} %all-reduce.6.cloned.1.call-done, f32[512]{0:T(512)S(1)} %add_rsqrt_fusion), kind=kOutput, calls=%fused_computation.6 | convolution fusion | flops 2422603264 | bytes 18092032 | tf_op jit(solution)/shard_map/dot_general | solution.py:67
  187.1 17.9 %all-reduce.1 = (f32[512]{0:T(512)S(1)}, f32[512]{0:T(512)S(1)}) all-reduce(f32[512]{0:T(512)S(1)} %get-tuple-element.20, f32[512]{0:T(512)S(1)} %get-tuple-element.22), channel_id=1, replica_groups=mesh['row'=16,'proto'=8] {'proto'}, use_global_device_ids=true, to_apply=%region_11.0 | all-reduce | flops 1024 | bytes 8192 | tf_op jit(solution)/shard_map/pmax | solution.py:70
  205.0 10.3 %exponential_reduce_fusion = (f32[512]{0:T(512)S(1)}, f32[512]{0:T(512)S(1)}) fusion(f32[512,6144]{1,0:T(8,128)} %get-tuple-element.21, f32[512]{0:T(512)S(1)} %get-tuple-element.14, f32[512]{0:T(512)S(1)} %get-tuple-element.15, f32[512,6144]{1,0:T(8,128)} %get-tuple-element.23, f32[6144]{0:T(1024)S(1)} %copy-done.3), kind=kLoop, calls=%fused_computation.4 | loop fusion | flops 22019072 | bytes 25198592 | tf_op jit(solution)/shard_map/reduce_sum | solution.py:73
  215.3 16.4 %all-reduce = (f32[512]{0:T(512)S(1)}, f32[512]{0:T(512)S(1)}) all-reduce(f32[512]{0:T(512)S(1)} %get-tuple-element.24, f32[512]{0:T(512)S(1)} %get-tuple-element.25), channel_id=1, replica_groups=mesh['row'=16,'proto'=8] {'proto'}, use_global_device_ids=true, to_apply=%region_13.0 | all-reduce | flops 1024 | bytes 8192 | tf_op jit(solution)/shard_map/psum | solution.py:73
  231.7 12.0 %multiply_convert_fusion = (bf16[512,6144]{1,0:T(8,128)(2,1)S(1)}, f32[512]{0:T(512)S(1)}) fusion(f32[512,6144]{1,0:T(8,128)} %get-tuple-element.21, f32[512]{0:T(512)S(1)} %get-tuple-element.12, f32[512]{0:T(512)S(1)} %broadcast_multiply_fusion, f32[512]{0:T(512)S(1)} %get-tuple-element.14, f32[512]{0:T(512)S(1)} %get-tuple-element.13, ...), kind=kLoop, calls=%fused_computation | loop fusion | flops 44039680 | bytes 31496192 | tf_op jit(solution)/shard_map/convert_element_type | solution.py:79
  243.7 2.7 copy-done.1
  246.3 6.7 fusion.15
  253.1 76.8 %all-reduce.8.cloned.1.call-done = f32[512,384]{1,0:T(8,128)} async-done(((f32[512,384]{1,0:T(8,128)}), f32[512,384]{1,0:T(8,128)}) %all-reduce.8.cloned.1.call-update) | async-done | bytes 786448 | tf_op jit(solution)/shard_map/psum | solution.py:84
  332.6 1.7 convolution_convert_fusion.1
  334.4 7.7 %convolution_convert_fusion = bf16[384,6144]{1,0:T(8,128)(2,1)} fusion(bf16[512,6144]{1,0:T(8,128)(2,1)} %copy-done.1, f32[512,384]{1,0:T(8,128)S(1)} %copy-done.2, f32[512]{0:T(512)S(1)} %add_rsqrt_fusion), kind=kOutput, calls=%fused_computation.10 | convolution fusion | flops 2418671616 | bytes 11798528 | tf_op jit(solution)/shard_map/dot_general | solution.py:19
  342.1 10.4 %convert_bitcast_fusion = bf16[4096,1024]{0,1:T(8,128)(2,1)} fusion(bf16[512,4096]{1,0:T(8,128)(2,1)} %param.8, f32[512,1024]{1,0:T(8,128)} %get-tuple-element.19, bf16[512,384]{1,0:T(8,128)(2,1)S(1)} %multiply_convert_fusion.2, bf16[1024,384]{1,0:T(8,128)(2,1)S(1)} %copy-done), kind=kOutput, calls=%fused_computation.11 | convolution fusion | flops 4707057664 | bytes 15859712 | tf_op jit(solution)/shard_map/dot_general | solution.py:19
  353.1 63.4 %psum.53 = f32[]{:T(128)} all-reduce(f32[]{:T(128)} %multiply_reduce_fusion.4), channel_id=1, replica_groups=mesh['row'=16,'proto'=8] {'row','proto'}, use_global_device_ids=true, to_apply=%region_16.0 | all-reduce | flops 1 | bytes 8 | tf_op jit(solution)/shard_map/psum | solution.py:78
  416.5 57.5 %all-reduce.10.cloned.1.call-done = bf16[1024,384]{1,0:T(8,128)(2,1)} async-done(((bf16[1024,384]{1,0:T(8,128)(2,1)}), bf16[1024,384]{1,0:T(8,128)(2,1)}) %all-reduce.10.cloned.1.call-update) | async-done | bytes 786448 | tf_op jit(solution)/shard_map/psum | solution.py:86
  474.0 2.4 convert_element_type.57
  476.4 85.6 %reduce-scatter.5.cloned.1.call-done = bf16[24,6144]{1,0:T(8,128)(2,1)} async-done(((bf16[384,6144]{1,0:T(8,128)(2,1)}), bf16[24,6144]{1,0:T(8,128)(2,1)}) %reduce-scatter.5.cloned.1.call-update) | async-done | bytes 294928 | tf_op jit(solution)/shard_map/reduce_scatter | solution.py:80
  561.9 1.8 convert_element_type.59
  563.7 103.1 %reduce-scatter.3.cloned.1.call-done = bf16[256,1024]{0,1:T(8,128)(2,1)} async-done(((bf16[4096,1024]{0,1:T(8,128)(2,1)}), bf16[256,1024]{0,1:T(8,128)(2,1)}) %reduce-scatter.3.cloned.1.call-update) | async-done | bytes 524304 | tf_op jit(solution)/shard_map/reduce_scatter | solution.py:88
  666.9 2.2 copy.13
  (32 shorter events, 10.6 us)
Async XLA Ops:
  7.2 89.0 %copy-start = (bf16[1024,384]{1,0:T(8,128)(2,1)S(1)}, bf16[1024,384]{1,0:T(8,128)(2,1)}, u32[]{:S(2)}) copy-start(bf16[1024,384]{1,0:T(8,128)(2,1)} %param.10) | copy-start | bytes 2359300
  7.2 78.4 %all-gather.2.cloned.1.call-start = ((), (), s32[]{:S(2)}) async-start(), calls=%async_computation.2 | async-start | bytes 8912896 | tf_op jit(solution)/shard_map/all_gather | solution.py:55
  7.9 167.3 %all-reduce.6.cloned.1.call-start = ((), (), s32[]{:S(2)}) async-start(), calls=%async_computation.3 | async-start | bytes 1572864 | tf_op jit(solution)/shard_map/psum | solution.py:60
  49.8 79.3 %copy-start.3 = (f32[6144]{0:T(1024)S(1)}, f32[6144]{0:T(1024)}, u32[]{:S(2)}) copy-start(f32[6144]{0:T(1024)} %param.14) | copy-start | bytes 73732
  97.8 232.1 %all-reduce.8.cloned.1.call-start = ((), (), s32[]{:S(2)}) async-start(), calls=%async_computation.4 | async-start | bytes 1572864 | tf_op jit(solution)/shard_map/psum | solution.py:84
  243.7 2.7 copy-start.1
  246.3 83.6 %copy-start.2 = (f32[512,384]{1,0:T(8,128)S(1)}, f32[512,384]{1,0:T(8,128)}, u32[]{:S(2)}) copy-start(f32[512,384]{1,0:T(8,128)} %all-reduce.6.cloned.1.call-done) | copy-start | bytes 2359300
  253.0 220.9 %all-reduce.10.cloned.1.call-start = ((), (), s32[]{:S(2)}) async-start(), calls=%async_computation.6 | async-start | bytes 1572864 | tf_op jit(solution)/shard_map/psum | solution.py:86
  334.3 227.6 %reduce-scatter.5.cloned.1.call-start = ((), (), s32[]{:S(2)}) async-start(), calls=%async_computation.7 | async-start | bytes 5013504 | tf_op jit(solution)/shard_map/reduce_scatter | solution.py:80
  342.1 324.8 %reduce-scatter.3.cloned.1.call-start = ((), (), s32[]{:S(2)}) async-start(), calls=%async_computation.5 | async-start | bytes 8912896 | tf_op jit(solution)/shard_map/reduce_scatter | solution.py:88
Sparse Core Ops, SparseCore 0:
  10.5 75.0 all-gather.1
  97.9 77.2 all-reduce.5
  253.2 76.7 all-reduce.7
  334.4 139.4 all-reduce.9
  477.9 83.9 reduce-scatter.4
  566.0 100.7 reduce-scatter.2
where the time goes:
time: 677 us; the launch traced here: 676 us
  waiting for transfers between devices  397 us (59%)
  blocking collectives  167 us (25%)
  matrix products  58.3 us (9%)
  other arithmetic  34.4 us (5%)
  between operations  14.2 us (2%)
    reduce_scatter x1, waiting for transfers between devices, on_device(): lax.psum_scatter(inner(tokens, dpre).astype(jnp.bfloat16), 'row', scatter...  103 us
    reduce_scatter x1, waiting for transfers between devices, on_device(): lax.psum_scatter(inner(student_n, grad_s).astype(jnp.bfloat16), 'row', sc...  85.6 us
    psum x1, waiting for transfers between devices, on_device(): dnorm = lax.psum(dnorm_part, 'proto')  76.8 us
    psum x1, blocking collectives, on_device(): loss = lax.psum(jnp.sum(weight * cross), ('row', 'proto'))  63.4 us
    psum x1, waiting for transfers between devices, on_device(): lax.psum(inner(hidden, dbott).astype(jnp.bfloat16), 'row')  57.5 us
    psum x1, blocking collectives, on_device(): counts = lax.psum(jnp.sum(onehot, axis=0), 'row')  38.4 us
    psum x1, waiting for transfers between devices, on_device(): bott = lax.psum(partial_value, 'proto')  37 us
    all_gather x1, waiting for transfers between devices, on_device(): lax.all_gather(w_in, 'row', axis=0, tiled=True)  35.8 us
  transfers between devices with their start and end apart: 6, of which 6 were waited for; matrix products, arithmetic and copies ran while one was open for 5% of the time, Pallas kernels for 0%

commit v1 on v0

--- a/solution.py
+++ b/solution.py
@@ -7,6 +7,11 @@
 tau_student = 0.1
 loss_scale = 1048576.0
 norm_eps = 1e-06
+
+
+def swapped_in(x, axis, along):
+    sent = jnp.stack([x] * lax.axis_size(axis))
+    return jnp.concatenate(lax.all_to_all(sent, axis, 0, 0), axis=along)
 
 
 def gelu_parts(values):
@@ -51,9 +56,7 @@
     onehot = (image_of[:, None] == jnp.arange(images, dtype=jnp.int32)[None, :]).astype(jnp.float32)
     counts = lax.psum(jnp.sum(onehot, axis=0), "row")
     weight = 1.0 / (images * jnp.sum(onehot * counts[None, :], axis=1))
-    pre = jnp.dot(
-        tokens, lax.all_gather(w_in, "row", axis=0, tiled=True), preferred_element_type=jnp.float32
-    )
+    pre = jnp.dot(tokens, swapped_in(w_in, "row", 0), preferred_element_type=jnp.float32)
     act, slope = gelu_parts(pre)
     hidden = act.astype(jnp.bfloat16)
     partial_value = jnp.dot(hidden, w_out, preferred_element_type=jnp.float32)

time: 677 us -> 764 us (1.13)
  blocking collectives: 167 us -> 282 us
  waiting for transfers between devices: 397 us -> 360 us
    psum x1, blocking collectives: 38.4 us -> 154 us  [on_device(): counts = lax.psum(jnp.sum(onehot, axis=0), 'row')]
    all_gather x1 -> x0, waiting for transfers between devices: 35.8 us -> none  [on_device(): lax.all_gather(w_in, 'row', axis=0, tiled=True)]
  transfers between devices with their start and end apart: 6 -> 6, of which waited for: 6 -> 5; matrix products, arithmetic and copies ran while one was open for 5% -> 4% of each run, Pallas kernels for 0% -> 0%
where the time goes in v1:
time: 764 us
  waiting for transfers between devices  360 us (47%)
  blocking collectives  282 us (37%)
  matrix products  58.3 us (8%)
  other arithmetic  31.5 us (4%)
  between operations  13.9 us (2%)
  local copies, waits for them, and re-layouts  10.3 us (1%)
    psum x1, blocking collectives, on_device(): counts = lax.psum(jnp.sum(onehot, axis=0), 'row')  154 us
    reduce_scatter x1, waiting for transfers between devices, on_device(): lax.psum_scatter(inner(tokens, dpre).astype(jnp.bfloat16), 'row', scatter...  103 us
    reduce_scatter x1, waiting for transfers between devices, on_device(): lax.psum_scatter(inner(student_n, grad_s).astype(jnp.bfloat16), 'row', sc...  85.6 us
    psum x1, waiting for transfers between devices, on_device(): dnorm = lax.psum(dnorm_part, 'proto')  76.8 us
    psum x1, blocking collectives, on_device(): loss = lax.psum(jnp.sum(weight * cross), ('row', 'proto'))  63.4 us
    psum x1, waiting for transfers between devices, on_device(): lax.psum(inner(hidden, dbott).astype(jnp.bfloat16), 'row')  57.5 us
    psum x1, waiting for transfers between devices, on_device(): bott = lax.psum(partial_value, 'proto')  36.8 us
    all_gather x1, blocking collectives, on_device(): lax.all_gather(teacher_norm(teacher_z), 'proto', axis=0, tiled=True)  31.2 us
  transfers between devices with their start and end apart: 6, of which 5 were waited for; matrix products, arithmetic and copies ran while one was open for 4% of the time, Pallas kernels for 0%

profile of v1, /device:TPU:0, one launch (start us, length us, event | category | flops | bytes accessed | tf_op | source)
XLA Modules:
  0.0 763.8 jit_solution(906880747237233244)
XLA Ops:
  7.2 5.4 stack.2
  12.6 7.3 all-to-all-start
  20.1 153.6 %psum.49 = f32[64]{0:T(128)S(1)} all-reduce(f32[64]{0:T(128)S(1)} %convert_reduce_fusion), channel_id=1, replica_groups=mesh['row'=16,'proto'=8] {'row'}, use_global_device_ids=true, to_apply=%region_1.0 | all-reduce | flops 64 | bytes 512 | tf_op jit(solution)/shard_map/psum | solution.py:57
  174.0 10.6 %multiply_convert_fusion.1 = (bf16[512,1024]{1,0:T(8,128)(2,1)S(1)}, f32[512,1024]{1,0:T(8,128)}) fusion(bf16[512,4096]{1,0:T(8,128)(2,1)} %param.8, bf16[4096,1024]{1,0:T(8,128)(2,1)} %bitcast), kind=kOutput, calls=%fused_computation.19 | convolution fusion | flops 4297588736 | bytes 15728640 | tf_op jit(solution)/shard_map/dot_general | solution.py:59
  186.3 31.2 %all_gather.3 = bf16[512,384]{1,0:T(8,128)(2,1)S(1)} all-gather(bf16[64,384]{1,0:T(8,128)(2,1)S(1)} %fusion.10), channel_id=1, replica_groups=mesh['row'=16,'proto'=8] {'proto'}, dimensions={0}, use_global_device_ids=true | all-gather | bytes 442368 | tf_op jit(solution)/shard_map/all_gather | solution.py:66
  217.5 9.0 %fusion = (f32[512]{0:T(512)S(1)}, f32[512,6144]{1,0:T(8,128)}) fusion(f32[6144]{0:T(1024)S(1)} %copy-done.4, bf16[512,384]{1,0:T(8,128)(2,1)S(1)} %all_gather.3, bf16[384,6144]{1,0:T(8,128)(2,1)} %param.13), kind=kOutput, calls=%fused_computation.7 | convolution fusion | flops 2425355776 | bytes 17721344 | tf_op jit(solution)/shard_map/dot_general | solution.py:68
  226.5 36.8 %all-reduce.6.cloned.1.call-done = f32[512,384]{1,0:T(8,128)} async-done(((f32[512,384]{1,0:T(8,128)}), f32[512,384]{1,0:T(8,128)}) %all-reduce.6.cloned.1.call-update) | async-done | bytes 786448 | tf_op jit(solution)/shard_map/psum | solution.py:63
  264.6 10.6 %multiply_reduce_fusion.1 = (f32[512]{0:T(512)S(1)}, f32[512,6144]{1,0:T(8,128)}) fusion(bf16[384,6144]{1,0:T(8,128)(2,1)} %param.12, f32[512,384]{1,0:T(8,128)} %all-reduce.6.cloned.1.call-done, f32[512]{0:T(512)S(1)} %add_rsqrt_fusion), kind=kOutput, calls=%fused_computation.6 | convolution fusion | flops 2422603264 | bytes 18092032 | tf_op jit(solution)/shard_map/dot_general | solution.py:70
  275.3 17.9 %all-reduce.1 = (f32[512]{0:T(512)S(1)}, f32[512]{0:T(512)S(1)}) all-reduce(f32[512]{0:T(512)S(1)} %get-tuple-element.20, f32[512]{0:T(512)S(1)} %get-tuple-element.22), channel_id=1, replica_groups=mesh['row'=16,'proto'=8] {'proto'}, use_global_device_ids=true, to_apply=%region_11.0 | all-reduce | flops 1024 | bytes 8192 | tf_op jit(solution)/shard_map/pmax | solution.py:73
  293.1 10.3 %exponential_reduce_fusion = (f32[512]{0:T(512)S(1)}, f32[512]{0:T(512)S(1)}) fusion(f32[512,6144]{1,0:T(8,128)} %get-tuple-element.21, f32[512]{0:T(512)S(1)} %get-tuple-element.14, f32[512]{0:T(512)S(1)} %get-tuple-element.15, f32[512,6144]{1,0:T(8,128)} %get-tuple-element.23, f32[6144]{0:T(1024)S(1)} %copy-done.4), kind=kLoop, calls=%fused_computation.4 | loop fusion | flops 22019072 | bytes 25198592 | tf_op jit(solution)/shard_map/reduce_sum | solution.py:76
  303.4 16.4 %all-reduce = (f32[512]{0:T(512)S(1)}, f32[512]{0:T(512)S(1)}) all-reduce(f32[512]{0:T(512)S(1)} %get-tuple-element.24, f32[512]{0:T(512)S(1)} %get-tuple-element.25), channel_id=1, replica_groups=mesh['row'=16,'proto'=8] {'proto'}, use_global_device_ids=true, to_apply=%region_13.0 | all-reduce | flops 1024 | bytes 8192 | tf_op jit(solution)/shard_map/psum | solution.py:76
  319.8 12.0 %multiply_convert_fusion = (bf16[512,6144]{1,0:T(8,128)(2,1)S(1)}, f32[512]{0:T(512)S(1)}) fusion(f32[512,6144]{1,0:T(8,128)} %get-tuple-element.21, f32[512]{0:T(512)S(1)} %get-tuple-element.12, f32[512]{0:T(512)S(1)} %broadcast_multiply_fusion, f32[512]{0:T(512)S(1)} %get-tuple-element.14, f32[512]{0:T(512)S(1)} %get-tuple-element.13, ...), kind=kLoop, calls=%fused_computation | loop fusion | flops 44039680 | bytes 31496192 | tf_op jit(solution)/shard_map/convert_element_type | solution.py:82
  331.8 2.7 copy-done.1
  334.4 6.7 fusion.15
  341.2 76.8 %all-reduce.8.cloned.1.call-done = f32[512,384]{1,0:T(8,128)} async-done(((f32[512,384]{1,0:T(8,128)}), f32[512,384]{1,0:T(8,128)}) %all-reduce.8.cloned.1.call-update) | async-done | bytes 786448 | tf_op jit(solution)/shard_map/psum | solution.py:87
  422.5 7.7 %convolution_convert_fusion = bf16[384,6144]{1,0:T(8,128)(2,1)} fusion(bf16[512,6144]{1,0:T(8,128)(2,1)} %copy-done.1, f32[512,384]{1,0:T(8,128)S(1)} %copy-done.2, f32[512]{0:T(512)S(1)} %add_rsqrt_fusion), kind=kOutput, calls=%fused_computation.10 | convolution fusion | flops 2418671616 | bytes 11798528 | tf_op jit(solution)/shard_map/dot_general | solution.py:24
  430.2 10.4 %convert_bitcast_fusion = bf16[4096,1024]{0,1:T(8,128)(2,1)} fusion(bf16[512,4096]{1,0:T(8,128)(2,1)} %param.8, f32[512,1024]{1,0:T(8,128)} %get-tuple-element.19, bf16[512,384]{1,0:T(8,128)(2,1)S(1)} %multiply_convert_fusion.2, bf16[1024,384]{1,0:T(8,128)(2,1)S(1)} %copy-done), kind=kOutput, calls=%fused_computation.11 | convolution fusion | flops 4707057664 | bytes 15859712 | tf_op jit(solution)/shard_map/dot_general | solution.py:24
  441.2 63.4 %psum.53 = f32[]{:T(128)} all-reduce(f32[]{:T(128)} %multiply_reduce_fusion.4), channel_id=1, replica_groups=mesh['row'=16,'proto'=8] {'row','proto'}, use_global_device_ids=true, to_apply=%region_16.0 | all-reduce | flops 1 | bytes 8 | tf_op jit(solution)/shard_map/psum | solution.py:81
  504.6 57.5 %all-reduce.10.cloned.1.call-done = bf16[1024,384]{1,0:T(8,128)(2,1)} async-done(((bf16[1024,384]{1,0:T(8,128)(2,1)}), bf16[1024,384]{1,0:T(8,128)(2,1)}) %all-reduce.10.cloned.1.call-update) | async-done | bytes 786448 | tf_op jit(solution)/shard_map/psum | solution.py:89
  562.1 2.4 convert_element_type.57
  564.5 85.6 %reduce-scatter.5.cloned.1.call-done = bf16[24,6144]{1,0:T(8,128)(2,1)} async-done(((bf16[384,6144]{1,0:T(8,128)(2,1)}), bf16[24,6144]{1,0:T(8,128)(2,1)}) %reduce-scatter.5.cloned.1.call-update) | async-done | bytes 294928 | tf_op jit(solution)/shard_map/reduce_scatter | solution.py:83
  650.1 1.8 convert_element_type.59
  651.9 103.1 %reduce-scatter.3.cloned.1.call-done = bf16[256,1024]{0,1:T(8,128)(2,1)} async-done(((bf16[4096,1024]{0,1:T(8,128)(2,1)}), bf16[256,1024]{0,1:T(8,128)(2,1)}) %reduce-scatter.3.cloned.1.call-update) | async-done | bytes 524304 | tf_op jit(solution)/shard_map/reduce_scatter | solution.py:91
  755.0 2.2 copy.13
  (36 shorter events, 8.6 us)
Async XLA Ops:
  7.2 177.5 %copy-start = (bf16[1024,384]{1,0:T(8,128)(2,1)S(1)}, bf16[1024,384]{1,0:T(8,128)(2,1)}, u32[]{:S(2)}) copy-start(bf16[1024,384]{1,0:T(8,128)(2,1)} %param.10) | copy-start | bytes 2359300
  12.6 7.4 copy-start.5
  12.6 161.1 %copy-start.3 = (bf16[64,384]{1,0:T(8,128)(2,1)S(1)}, bf16[64,384]{1,0:T(8,128)(2,1)}, u32[]{:S(2)}) copy-start(bf16[64,384]{1,0:T(8,128)(2,1)} %param.11) | copy-start | bytes 147460
  12.6 161.4 %all-to-all-start = ((bf16[16,256,1024]{2,1,0:T(8,128)(2,1)}), bf16[16,256,1024]{2,1,0:T(8,128)(2,1)}, u32[]{:S(2)}, u32[]{:S(2)}) async-start(bf16[16,256,1024]{2,1,0:T(8,128)(2,1)} %stack.2), calls=%async_computation | async-start | bytes 16777216 | tf_op jit(solution)/shard_map/all_to_all | solution.py:14
  19.9 243.4 %all-reduce.6.cloned.1.call-start = ((), (), s32[]{:S(2)}) async-start(), calls=%async_computation.3 | async-start | bytes 1572864 | tf_op jit(solution)/shard_map/psum | solution.py:63
  174.0 43.5 %copy-start.4 = (f32[6144]{0:T(1024)S(1)}, f32[6144]{0:T(1024)}, u32[]{:S(2)}) copy-start(f32[6144]{0:T(1024)} %param.14) | copy-start | bytes 73732
  186.2 231.8 %all-reduce.8.cloned.1.call-start = ((), (), s32[]{:S(2)}) async-start(), calls=%async_computation.4 | async-start | bytes 1572864 | tf_op jit(solution)/shard_map/psum | solution.py:87
  331.8 2.7 copy-start.1
  334.4 83.6 %copy-start.2 = (f32[512,384]{1,0:T(8,128)S(1)}, f32[512,384]{1,0:T(8,128)}, u32[]{:S(2)}) copy-start(f32[512,384]{1,0:T(8,128)} %all-reduce.6.cloned.1.call-done) | copy-start | bytes 2359300
  341.2 220.9 %all-reduce.10.cloned.1.call-start = ((), (), s32[]{:S(2)}) async-start(), calls=%async_computation.6 | async-start | bytes 1572864 | tf_op jit(solution)/shard_map/psum | solution.py:89
  422.4 227.6 %reduce-scatter.5.cloned.1.call-start = ((), (), s32[]{:S(2)}) async-start(), calls=%async_computation.7 | async-start | bytes 5013504 | tf_op jit(solution)/shard_map/reduce_scatter | solution.py:83
  430.2 324.8 %reduce-scatter.3.cloned.1.call-start = ((), (), s32[]{:S(2)}) async-start(), calls=%async_computation.5 | async-start | bytes 8912896 | tf_op jit(solution)/shard_map/reduce_scatter | solution.py:91
Sparse Core Ops, SparseCore 0:
  186.4 76.8 all-reduce.5
  341.3 76.7 all-reduce.7
  422.6 139.4 all-reduce.9
  566.1 83.9 reduce-scatter.4
  654.2 100.7 reduce-scatter.2
